TPU v7x, 128 devices: a whole 4x4x4 slice. The times are simulated.
128 devices in a mesh: blk: 16 (over y_hi, x, core), kv: 8 (over z, y_lo).
Axes of the slice: x: 4, y: 4 (y_hi: 2, y_lo: 2; y = y_hi * 2 + y_lo), z: 4, core: 2. Of those that a mesh axis runs over, the one named last changes fastest.
Arguments:
- tokens: bfloat16 [8192, 2560], P('blk'), may hold values from -6 to 6
- attn_gain: float32 [2560], replicated, may hold values from 0.1 to 1.9
- mlp_gain: float32 [2560], replicated, may hold values from 0.1 to 1.9
- w_query: float32 [2560, 2560], P(('blk', 'kv')), may hold values from -0.375 to 0.375
- w_key: float32 [2560, 640], P(('blk', 'kv')), may hold values from -0.125 to 0.125
- w_value: float32 [2560, 640], P(('blk', 'kv')), may hold values from -0.125 to 0.125
- w_gate: float32 [2560, 6912], P(('blk', 'kv')), may hold values from -0.125 to 0.125
- w_up: float32 [2560, 6912], P(('blk', 'kv')), may hold values from -0.125 to 0.125
- w_out: bfloat16 [2560, 2560], P('kv'), may hold values from -0.125 to 0.125
- w_down: bfloat16 [6912, 2560], P('kv'), may hold values from -0.078125 to 0.078125
- cache: bfloat16 [2, 128, 8, 80, 128], P(None, 'blk', 'kv'), may hold values from -300 to 300
- slot_prompt: int32 [128], replicated, may hold values from 0 to 15, as said below
- prefix_len: int32 [16], replicated, may hold values from 1 to 4096, as said below
- new_len: int32 [16], replicated, may hold values from 256 to 512, as said below
Outputs:
- mixed: bfloat16 [8192, 2560], P('blk', 'kv')
Inputs may be any that keep to these rules, and one draw needn't show every extreme that they name: `slot_prompt`: the 8 slots of one index of blk hold at most 2 blocks of one prompt. One prompt, drawn afresh, has exactly 2 blocks on every index of blk; the other 6 slots of an index hold blocks of distinct prompts; every prompt has at least one block. `prefix_len`: A prompt with c slots has a prefix longer than (c - 1) * 128 and at most c * 128. Rows i >= new_len[p] of prompt p are padding.
All inputs are finite; a program needn't handle non-finite values.
Results may differ from a plain program's by a relative error of at most 0.019.
The roundings to bfloat16 on the way count: a program that leaves them out, or rounds other values in their place, can miss the bound.
Values may be sent and summed in bfloat16 or wider, within the bound.
A program may use at most 128 MiB of HBM per device.

v0:
```python
import math
import jax
import jax.numpy as jnp
from jax import lax
from jax.sharding import PartitionSpec as P

HEADS = 32
KV_HEADS = 8
HD = 80
WINDOW = 4096
SINKS = 4
BLOCK = 128
CAP = 2
FLOOR_SCORE = -1e30
EPSILON = 1e-05
ROPE_BASE = 10000.0


def rms_scale(row_data, gain_vec):
    values = row_data.astype(jnp.float32)
    mean_square = jnp.mean(values * values, axis=-1, keepdims=True)
    return (values * lax.rsqrt(mean_square + EPSILON) * gain_vec).astype(jnp.bfloat16)


def rotate(values, positions):
    head_width = values.shape[-1]
    half_width = head_width // 2
    frequency = ROPE_BASE ** (-2.0 * jnp.arange(half_width, dtype=jnp.float32) / head_width)
    angles = positions.astype(jnp.float32)[:, None] * frequency[None, :]
    cosine = jnp.cos(angles)[:, None, :]
    sine_wave = jnp.sin(angles)[:, None, :]
    first_half = values[..., :half_width]
    second_half = values[..., half_width:]
    return jnp.concatenate(
        [
            first_half * cosine - second_half * sine_wave,
            second_half * cosine + first_half * sine_wave,
        ],
        axis=-1,
    )


def slot_ranks(slot_prompt, prompts, slots):
    onehot = (slot_prompt[:, None] == jnp.arange(prompts, dtype=jnp.int32)[None, :]).astype(
        jnp.int32
    )
    running = jnp.cumsum(onehot, axis=0)
    global_rank = jnp.sum(onehot * (running - 1), axis=1)
    local_count = jnp.cumsum(onehot.reshape(-1, slots, prompts), axis=1).reshape(-1, prompts)
    local_rank = jnp.sum(onehot * (local_count - 1), axis=1)
    return (global_rank, local_rank)


def visible(query_pos, key_pos):
    distance = query_pos - key_pos
    return (distance >= 0) & ((distance < WINDOW) | (key_pos < SINKS))


def partial_block(scores, seen_mask):
    masked = jnp.where(seen_mask, scores, FLOOR_SCORE)
    row_max = jnp.max(masked, axis=-1)
    weights = jnp.where(seen_mask, jnp.exp(masked - row_max[..., None]), 0.0)
    return (row_max, jnp.sum(weights, axis=-1), weights.astype(jnp.bfloat16))


def combine(first_part, second_part):
    maxima = jnp.maximum(first_part[0], second_part[0])
    scale_first = jnp.exp(first_part[0] - maxima)
    scale_second = jnp.exp(second_part[0] - maxima)
    totals = first_part[1] * scale_first + second_part[1] * scale_second
    outputs = first_part[2] * scale_first[..., None] + second_part[2] * scale_second[..., None]
    return (maxima, totals, outputs)


def pack_groups(matrices, groups):
    pieces = [
        matrix.reshape(matrix.shape[0], groups, matrix.shape[1] // groups) for matrix in matrices
    ]
    joined = jnp.concatenate(pieces, axis=2)
    return joined.reshape(matrices[0].shape[0], -1).astype(jnp.bfloat16)


def restack(moved_rows, groups, n_blocks):
    columns = moved_rows.shape[1]
    ordered = moved_rows.reshape(groups, n_blocks, -1, columns)
    return jnp.transpose(ordered, (1, 0, 2, 3)).reshape(-1, columns)


def shards(
    tokens,
    attn_gain,
    mlp_gain,
    w_query,
    w_key,
    w_value,
    w_gate,
    w_up,
    w_out,
    w_down,
    cache,
    slot_prompt,
    prefix_len,
    new_len,
):
    groups = lax.axis_size("kv")
    n_blocks = lax.axis_size("blk")
    blk_index = lax.axis_index("blk")
    kv_index = lax.axis_index("kv")
    merged_attn = pack_groups((w_query, w_key, w_value), groups)
    merged_mlp = pack_groups((w_gate, w_up), groups)
    collected = (
        lax.all_gather(merged_attn, "blk", axis=0, tiled=True),
        lax.all_gather(merged_mlp, "blk", axis=0, tiled=True),
    )
    moved_attn, moved_mlp = (
        lax.all_to_all(collected[0], "kv", split_axis=1, concat_axis=0, tiled=True),
        lax.all_to_all(collected[1], "kv", split_axis=1, concat_axis=0, tiled=True),
    )
    w_qkv = restack(moved_attn, groups, n_blocks)
    w_pair = restack(moved_mlp, groups, n_blocks)
    query_width = w_query.shape[1] // groups
    key_width = w_key.shape[1] // groups
    kv_local = key_width // HD
    per_group = HEADS // KV_HEADS
    new_rows = tokens.shape[0]
    prompts = prefix_len.shape[0]
    slots = cache.shape[1]
    score_scale = 1.0 / math.sqrt(HD)
    prefix_here = prefix_len[blk_index]
    live_count = new_len[blk_index]
    row_ids = jnp.arange(new_rows, dtype=jnp.int32)
    positions = prefix_here + row_ids
    offsets = jnp.arange(BLOCK, dtype=jnp.int32)
    normed = rms_scale(tokens, attn_gain)
    projected = jnp.dot(normed, w_qkv, preferred_element_type=jnp.float32)
    queries = rotate(projected[:, :query_width].reshape(new_rows, -1, HD), positions).astype(
        jnp.bfloat16
    )
    key_new = rotate(
        projected[:, query_width : query_width + key_width].reshape(new_rows, kv_local, HD),
        positions,
    ).astype(jnp.bfloat16)
    value_new = (
        projected[:, query_width + key_width :].reshape(new_rows, kv_local, HD).astype(jnp.bfloat16)
    )
    grouped_q = queries.reshape(new_rows, kv_local, per_group, HD)
    own_scores = (
        jnp.einsum("qgnd,kgd->gnqk", grouped_q, key_new, preferred_element_type=jnp.float32)
        * score_scale
    )
    own_mask = (row_ids[None, :] < live_count) & visible(positions[:, None], positions[None, :])
    own_max, own_sum, own_weights = partial_block(own_scores, own_mask)
    own_out = jnp.einsum(
        "gnqk,kgd->gnqd", own_weights, value_new, preferred_element_type=jnp.float32
    )
    running = (own_max, own_sum, own_out)
    global_rank, local_rank = slot_ranks(slot_prompt, prompts, slots)
    own_prompts = lax.dynamic_slice_in_dim(slot_prompt, blk_index * slots, slots)
    own_ranks = lax.dynamic_slice_in_dim(local_rank, blk_index * slots, slots)
    placed = own_prompts * CAP + own_ranks
    buffer_ids = jnp.arange(prompts * CAP, dtype=jnp.int32)
    matches = placed[None, :] == buffer_ids[:, None]
    source_slot = jnp.sum(
        jnp.where(matches, jnp.arange(slots, dtype=jnp.int32)[None, :], 0), axis=1
    )
    filled = jnp.any(matches, axis=1)
    outgoing = jnp.where(
        filled[None, :, None, None, None],
        jnp.take(cache, source_slot, axis=1),
        jnp.zeros((), cache.dtype),
    )
    arrived = lax.all_to_all(outgoing, "blk", split_axis=1, concat_axis=1, tiled=True)
    slot_ids = jnp.arange(prompts * slots, dtype=jnp.int32)
    landing = slot_ids // slots * CAP + local_rank
    for_me = slot_prompt == blk_index
    received = (landing[None, :] == buffer_ids[:, None]) & for_me[None, :]
    block_number = jnp.sum(jnp.where(received, global_rank[None, :], 0), axis=1)
    block_live = jnp.any(received, axis=1)
    total_slots = prompts * CAP
    group_slots = min(total_slots, max(1, 512 // BLOCK))
    step_count = total_slots // group_slots
    key_blocks = arrived[0].reshape(step_count, group_slots, kv_local, HD, BLOCK)
    value_blocks = arrived[1].reshape(step_count, group_slots, kv_local, HD, BLOCK)
    numbers = block_number.reshape(step_count, group_slots)
    live_flags = block_live.reshape(step_count, group_slots)

    def prefix_step(running_state, inputs):
        key_part, value_part, number_part, flag_part = inputs
        scores = (
            jnp.einsum("qgnd,sgdt->gnqst", grouped_q, key_part, preferred_element_type=jnp.float32)
            * score_scale
        )
        scores = scores.reshape(kv_local, per_group, new_rows, group_slots * BLOCK)
        key_pos = number_part[:, None] * BLOCK + offsets[None, :]
        key_live = (flag_part[:, None] & (key_pos < prefix_here)).reshape(-1)
        seen_mask = key_live[None, :] & visible(positions[:, None], key_pos.reshape(-1)[None, :])
        block_max, block_sum, weights = partial_block(scores, seen_mask)
        weights = weights.reshape(kv_local, per_group, new_rows, group_slots, BLOCK)
        block_out = jnp.einsum(
            "gnqst,sgdt->gnqd", weights, value_part, preferred_element_type=jnp.float32
        )
        return (combine(running_state, (block_max, block_sum, block_out)), None)

    running = lax.scan(prefix_step, running, (key_blocks, value_blocks, numbers, live_flags))[0]
    totals = running[1]
    outputs = running[2]
    attended = (
        jnp.transpose(outputs / totals[..., None], (2, 0, 1, 3))
        .reshape(new_rows, -1)
        .astype(jnp.bfloat16)
    )
    projected_out = jnp.dot(attended, w_out, preferred_element_type=jnp.float32)
    summed = lax.psum(projected_out.astype(jnp.bfloat16), "kv").astype(jnp.float32)
    middle = (tokens.astype(jnp.float32) + summed).astype(jnp.bfloat16)
    normed_mid = rms_scale(middle, mlp_gain)
    paired = jnp.dot(normed_mid, w_pair, preferred_element_type=jnp.float32)
    hidden_width = w_pair.shape[1] // 2
    hidden = (jax.nn.silu(paired[:, :hidden_width]) * paired[:, hidden_width:]).astype(jnp.bfloat16)
    down_part = jnp.dot(hidden, w_down, preferred_element_type=jnp.float32)
    reduced = lax.psum_scatter(
        down_part.astype(jnp.bfloat16), "kv", scatter_dimension=1, tiled=True
    ).astype(jnp.float32)
    out_width = reduced.shape[1]
    residual = lax.dynamic_slice_in_dim(middle, kv_index * out_width, out_width, 1).astype(
        jnp.float32
    )
    mixed = jnp.where((row_ids < live_count)[:, None], residual + reduced, 0.0)
    return mixed.astype(jnp.bfloat16)


def solution(mesh):
    return jax.shard_map(
        shards,
        mesh=mesh,
        in_specs=(
            P("blk", None),
            P(),
            P(),
            P(("blk", "kv"), None),
            P(("blk", "kv"), None),
            P(("blk", "kv"), None),
            P(("blk", "kv"), None),
            P(("blk", "kv"), None),
            P("kv", None),
            P("kv", None),
            P(None, "blk", "kv", None, None),
            P(),
            P(),
            P(),
        ),
        out_specs=P("blk", "kv"),
        check_vma=False,
    )
```

profile of v0, /device:TPU:1, one launch (start us, length us, event | category | flops | bytes accessed | tf_op | source)
XLA Modules:
  0.0 535.5 jit_solution(12732997169242167067)
XLA Ops:
  18.9 8.4 %all-to-all-start.1 = ((bf16[2,32,1,80,128]{4,3,0,2,1:T(8,128)(2,1)}), bf16[2,32,1,80,128]{4,3,0,2,1:T(8,128)(2,1)S(1)}, u32[]{:S(2)}, u32[]{:S(2)}) async-start(bf16[2,32,1,80,128]{4,3,0,2,1:T(8,128)(2,1)} %fusion.68), calls=%async_computation.1 | async-start | bytes 2621440 | tf_op jit(solution)/shard_map/all_to_all | solution.py:172
  27.4 41.5 %all-gather.5.cloned.1.call-done = bf16[16,20,3840]{2,1,0:T(8,128)(2,1)} async-done(((bf16[1,20,3840]{2,1,0:T(8,128)(2,1)}), bf16[16,20,3840]{2,1,0:T(8,128)(2,1)}) %all-gather.5.cloned.1.call-update) | async-done | bytes 2457616 | tf_op jit(solution)/shard_map/all_gather | solution.py:112
  68.9 6.6 %all_to_all.27 = bf16[320,8,480]{2,1,0:T(8,128)(2,1)} reshape(bf16[16,20,3840]{2,1,0:T(8,128)(2,1)} %all-gather.5.cloned.1.call-done) | data formatting | bytes 4915200 | tf_op jit(solution)/shard_map/all_to_all | solution.py:116
  75.4 4.2 copy.61
  79.6 4.7 all-to-all-start
  85.6 4.4 copy.60
  97.2 29.5 %all-to-all-done = bf16[320,8,480]{2,0,1:T(8,128)(2,1)} async-done(((bf16[320,8,480]{2,0,1:T(8,128)(2,1)}), bf16[320,8,480]{2,0,1:T(8,128)(2,1)}, u32[]{:S(2)}, u32[]{:S(2)}) %all-to-all-start) | async-done | bytes 2457632 | tf_op jit(solution)/shard_map/all_to_all | solution.py:116
  126.7 3.3 copy.62
  132.9 5.5 %reshape.470 = bf16[2560,480]{1,0:T(8,128)(2,1)} reshape(bf16[16,8,20,480]{3,2,1,0:T(8,128)(2,1)} %copy.63) | data formatting | bytes 4915200 | tf_op jit(solution)/shard_map/reshape | solution.py:86
  138.4 4.2 fusion.55
  146.5 16.6 %all-gather.7.cloned.1.call-done = bf16[16,20,13824]{2,1,0:T(8,128)(2,1)} async-done(((bf16[1,20,13824]{2,1,0:T(8,128)(2,1)}), bf16[16,20,13824]{2,1,0:T(8,128)(2,1)}) %all-gather.7.cloned.1.call-update) | async-done | bytes 8847376 | tf_op jit(solution)/shard_map/all_gather | solution.py:113
  163.1 16.9 %all_to_all.31 = bf16[320,8,1728]{2,1,0:T(8,128)(2,1)} reshape(bf16[16,20,13824]{2,1,0:T(8,128)(2,1)} %all-gather.7.cloned.1.call-done) | data formatting | bytes 17694720 | tf_op jit(solution)/shard_map/all_to_all | solution.py:117
  180.0 8.9 %copy.68 = bf16[320,8,1728]{2,0,1:T(8,128)(2,1)} copy(bf16[320,8,1728]{2,1,0:T(8,128)(2,1)} %all_to_all.31) | data formatting | bytes 17694720 | tf_op jit(solution)/shard_map/all_to_all | solution.py:117
  189.0 5.0 all-to-all-start.2
  194.0 57.9 %while.16 = (s32[]{:T(128)}, f32[1,4,512]{2,1,0:T(4,128)S(1)}, f32[1,4,512]{2,1,0:T(4,128)S(1)}, f32[1,4,512,80]{2,3,1,0:T(8,128)S(1)}, pred[8,4]{1,0:T(8,128)(4...) while((s32[]{:T(128)}, f32[1,4,512]{2,1,0:T(4,128)S(1)}, ...), condition=%wide.region_14.15_spmd.clone.clone, body=%wide.region_11.14_spmd.clone.clone.sunk | while | flops 351253504 | bytes 15599833 | solution.py:204
  252.0 3.1 convolution_convert_fusion.1
  255.3 151.3 %all-reduce.2.cloned.1.call-done = bf16[512,2560]{0,1:T(8,128)(2,1)} async-done(((bf16[512,2560]{0,1:T(8,128)(2,1)}), bf16[512,2560]{0,1:T(8,128)(2,1)}) %all-reduce.2.cloned.1.call-update) | async-done | bytes 2621456 | tf_op jit(solution)/shard_map/psum | solution.py:213
  406.6 5.1 fusion.44
  411.7 12.2 %copy.69 = bf16[320,8,1728]{2,1,0:T(8,128)(2,1)} copy(bf16[320,8,1728]{2,0,1:T(8,128)(2,1)} %all-to-all-done.2) | data formatting | bytes 17694720 | tf_op jit(solution)/shard_map/all_to_all | solution.py:117
  423.9 10.4 %copy.70 = bf16[16,8,20,1728]{3,2,1,0:T(8,128)(2,1)} copy(bf16[16,8,20,1728]{3,1,2,0:T(8,128)(2,1)} %bitcast.203) | data formatting | bytes 17694720 | tf_op jit(solution)/shard_map/transpose | solution.py:86
  434.3 14.4 %reshape.479 = bf16[2560,1728]{1,0:T(8,128)(2,1)} reshape(bf16[16,8,20,1728]{3,2,1,0:T(8,128)(2,1)} %copy.70) | data formatting | bytes 17694720 | tf_op jit(solution)/shard_map/reshape | solution.py:86
  448.6 8.9 %fusion.57 = f32[512,1728]{0,1:T(8,128)S(1)} fusion(bf16[2560,1728]{1,0:T(8,128)(2,1)} %reshape.479, bf16[512,2560]{0,1:T(8,128)(2,1)} %get-tuple-element.184, f32[2560]{0:T(1024)S(1)} %copy-done.4, f32[512]{0:T(512)S(1)} %add_rsqrt_fusion), kind=kOutput, calls=%fused_computation.68 | convolution fusion | flops 4535091200 | bytes 15020032 | tf_op jit(solution)/shard_map/dot_general | solution.py:216
  457.5 7.4 %fusion.51 = bf16[2560,512]{1,0:T(8,128)(2,1)} fusion(bf16[864,2560]{1,0:T(8,128)(2,1)} %param.25, f32[512,1728]{0,1:T(8,128)S(1)} %fusion.57), kind=kOutput, calls=%fused_computation.63 | convolution fusion | flops 2268889088 | bytes 10584064 | tf_op jit(solution)/shard_map/dot_general | solution.py:219
  465.0 61.9 %reduce-scatter.4.cloned.1.call-done = bf16[320,512]{1,0:T(8,128)(2,1)} async-done(((bf16[2560,512]{1,0:T(8,128)(2,1)}), bf16[320,512]{1,0:T(8,128)(2,1)}) %reduce-scatter.4.cloned.1.call-update) | async-done | bytes 327696
  (178 shorter events, 87.0 us)
Async XLA Ops:
  6.5 245.4 %copy-start = (bf16[320,2560]{1,0:T(8,128)(2,1)S(1)}, bf16[320,2560]{1,0:T(8,128)(2,1)}, u32[]{:S(2)}) copy-start(bf16[320,2560]{1,0:T(8,128)(2,1)} %param.24) | copy-start | bytes 4915204
  6.5 9.2 %copy-start.2 = (s32[128]{0:T(128)S(1)}, s32[128]{0:T(128)}, u32[]{:S(2)}) copy-start(s32[128]{0:T(128)} %param.27) | copy-start | bytes 1540
  6.5 62.3 %all-gather.5.cloned.1.call-start = ((), (), s32[]{:S(2)}) async-start(), calls=%async_computation.5 | async-start | bytes 3133440 | tf_op jit(solution)/shard_map/all_gather | solution.py:112
  7.5 9.2 %copy-start.1 = (bf16[2,8,1,80,128]{4,3,2,1,0:T(8,128)(2,1)S(1)}, bf16[2,8,1,80,128]{4,3,2,1,0:T(8,128)(2,1)}, u32[]{:S(2)}) copy-start(bf16[2,8,1,80,128]{4,3,2,1,0:T(8,128)(2,1)} %param.26) | copy-start | bytes 983044
  10.8 152.4 %all-gather.7.cloned.1.call-start = ((), (), s32[]{:S(2)}) async-start(), calls=%async_computation.6 | async-start | bytes 11280384 | tf_op jit(solution)/shard_map/all_gather | solution.py:113
  18.9 60.7 %all-to-all-start.1 = ((bf16[2,32,1,80,128]{4,3,0,2,1:T(8,128)(2,1)}), bf16[2,32,1,80,128]{4,3,0,2,1:T(8,128)(2,1)S(1)}, u32[]{:S(2)}, u32[]{:S(2)}) async-start(bf16[2,32,1,80,128]{4,3,0,2,1:T(8,128)(2,1)} %fusion.68), calls=%async_computation.1 | async-start | bytes 2621440 | tf_op jit(solution)/shard_map/all_to_all | solution.py:172
  75.4 8.9 %copy-start.5 = (s32[16]{0:T(128)S(1)}, s32[16]{0:T(128)}, u32[]{:S(2)}) copy-start(s32[16]{0:T(128)} %param.28) | copy-start | bytes 196
  75.4 9.6 %copy-start.6 = (s32[16]{0:T(128)S(1)}, s32[16]{0:T(128)}, u32[]{:S(2)}) copy-start(s32[16]{0:T(128)} %param.29) | copy-start | bytes 196
  79.6 47.1 %all-to-all-start = ((bf16[320,8,480]{2,0,1:T(8,128)(2,1)}), bf16[320,8,480]{2,0,1:T(8,128)(2,1)}, u32[]{:S(2)}, u32[]{:S(2)}) async-start(bf16[320,8,480]{2,0,1:T(8,128)(2,1)} %copy.61), calls=%async_computation | async-start | bytes 5242880 | tf_op jit(solution)/shard_map/all_to_all | solution.py:116
  132.9 5.5 %copy-start.3 = (f32[2560]{0:T(1024)S(1)}, f32[2560]{0:T(1024)}, u32[]{:S(2)}) copy-start(f32[2560]{0:T(1024)} %param.17) | copy-start | bytes 30724
  189.0 222.7 %all-to-all-start.2 = ((bf16[320,8,1728]{2,0,1:T(8,128)(2,1)}), bf16[320,8,1728]{2,0,1:T(8,128)(2,1)}, u32[]{:S(2)}, u32[]{:S(2)}) async-start(bf16[320,8,1728]{2,0,1:T(8,128)(2,1)} %copy.68), calls=%async_computation.2 | async-start | bytes 18350080 | tf_op jit(solution)/shard_map/all_to_all | solution.py:117
  194.0 212.6 %all-reduce.2.cloned.1.call-start = ((), (), s32[]{:S(2)}) async-start(), calls=%async_computation.4 | async-start | bytes 5242880 | tf_op jit(solution)/shard_map/psum | solution.py:213
  255.1 271.7 %reduce-scatter.4.cloned.1.call-start = ((), (), s32[]{:S(2)}) async-start(), calls=%async_computation.7 | async-start | bytes 2949120
  434.3 14.4 %copy-start.4 = (f32[2560]{0:T(1024)S(1)}, f32[2560]{0:T(1024)}, u32[]{:S(2)}) copy-start(f32[2560]{0:T(1024)} %param.18) | copy-start | bytes 30724
Sparse Core Ops, SparseCore 0:
  10.9 57.9 all-gather.4
  71.3 91.7 all-gather.6
  255.2 151.3 all-reduce.1
  465.1 61.6 reduce-scatter.3
where the time goes:
time: 543 us; the launch traced here: 536 us
  waiting for transfers between devices  301 us (55%)
  local copies, waits for them, and re-layouts  97.1 us (18%)
  matrix products  58.8 us (11%)
  other arithmetic  46.1 us (8%)
  starting transfers between devices  18.5 us (3%)
  between operations  13.6 us (3%)
    psum x1, waiting for transfers between devices, shards(): lax.psum(projected_out.astype(jnp.bfloat16), 'kv').astype(jnp.float32)  151 us
    unnamed x5, waiting for transfers between devices  61.9 us
    all_gather x1, waiting for transfers between devices, shards(): lax.all_gather(merged_attn, 'blk', axis=0, tiled=True)  41.5 us
    all_to_all x3, local copies, waits for them, and re-layouts, shards(): lax.all_to_all(collected[1], 'kv', split_axis=1, concat_axis=0, tiled=True)  38 us
    all_to_all x1, waiting for transfers between devices, shards(): lax.all_to_all(collected[0], 'kv', split_axis=1, concat_axis=0, tiled=True)  29.5 us
    reshape x2, local copies, waits for them, and re-layouts, restack(): return jnp.transpose(ordered, (1, 0, 2, 3)).reshape(-1, columns)  19.9 us
    dot_general x8, matrix products, prefix_step(): jnp.einsum('gnqst,sgdt->gnqd', weights, value_part, preferred_element_typ...  18.6 us
    all_gather x1, waiting for transfers between devices, shards(): lax.all_gather(merged_mlp, 'blk', axis=0, tiled=True)  16.6 us
  transfers between devices with their start and end apart: 7, of which 5 were waited for; matrix products, arithmetic and copies ran while one was open for 21% of the time, Pallas kernels for 0%

commit v1 on v0

--- a/solution.py
+++ b/solution.py
@@ -210,7 +210,9 @@
         .astype(jnp.bfloat16)
     )
     projected_out = jnp.dot(attended, w_out, preferred_element_type=jnp.float32)
-    summed = lax.psum(projected_out.astype(jnp.bfloat16), "kv").astype(jnp.float32)
+    summed = jnp.sum(lax.all_gather(projected_out.astype(jnp.bfloat16), "kv"), axis=0).astype(
+        jnp.float32
+    )
     middle = (tokens.astype(jnp.float32) + summed).astype(jnp.bfloat16)
     normed_mid = rms_scale(middle, mlp_gain)
     paired = jnp.dot(normed_mid, w_pair, preferred_element_type=jnp.float32)

time: 543 us -> 836 us (1.54)
  blocking collectives: 0 us -> 207 us
  waiting for transfers between devices: 301 us -> 367 us
  local copies, waits for them, and re-layouts: 97.1 us -> 111 us
  other arithmetic: 46.1 us -> 58.1 us
    all_gather x0 -> x1, waiting for transfers between devices: none -> 234 us  [shards(): lax.all_gather(projected_out.astype(jnp.bfloat16), 'kv')]
    all_to_all x0 -> x1, blocking collectives: none -> 207 us  [shards(): lax.all_to_all(collected[1], 'kv', split_axis=1, concat_axis=0, tiled=True)]
    psum x1 -> x0, waiting for transfers between devices: 151 us -> none  [shards(): lax.psum(projected_out.astype(jnp.bfloat16), 'kv').astype(jnp.float32)]
    reduce_scatter x0 -> x1, waiting for transfers between devices: none -> 63.4 us  [shards(): lax.psum_scatter(down_part.astype(jnp.bfloat16), 'kv', scatter_dimension=...]
    unnamed x5 -> x4, waiting for transfers between devices: 61.9 us -> 0.07 us
    all_gather x1, waiting for transfers between devices: 16.6 us -> 0.02 us  [shards(): lax.all_gather(merged_mlp, 'blk', axis=0, tiled=True)]
    reduce_sum x0 -> x1, other arithmetic: none -> 13.1 us  [shards(): jnp.sum(lax.all_gather(projected_out.astype(jnp.bfloat16), 'kv'), axis=0)]
  transfers between devices with their start and end apart: 7 -> 6, of which waited for: 5 -> 4; matrix products, arithmetic and copies ran while one was open for 21% -> 19% of each run, Pallas kernels for 0% -> 0%
where the time goes in v1:
time: 836 us; the launch traced here: 829 us
  waiting for transfers between devices  367 us (44%)
  blocking collectives  207 us (25%)
  local copies, waits for them, and re-layouts  111 us (13%)
  other arithmetic  58.1 us (7%)
  matrix products  57.6 us (7%)
  between operations  13.7 us (2%)
  starting transfers between devices  13.4 us (2%)
    all_gather x1, waiting for transfers between devices, shards(): lax.all_gather(projected_out.astype(jnp.bfloat16), 'kv')  234 us
    all_to_all x1, blocking collectives, shards(): lax.all_to_all(collected[1], 'kv', split_axis=1, concat_axis=0, tiled=True)  207 us
    reduce_scatter x1, waiting for transfers between devices, shards(): lax.psum_scatter(down_part.astype(jnp.bfloat16), 'kv', scatter_dimension=...  63.4 us
    all_gather x1, waiting for transfers between devices, shards(): lax.all_gather(merged_attn, 'blk', axis=0, tiled=True)  40.8 us
    all_to_all x3, local copies, waits for them, and re-layouts, shards(): lax.all_to_all(collected[1], 'kv', split_axis=1, concat_axis=0, tiled=True)  37.8 us
    all_to_all x1, waiting for transfers between devices, shards(): lax.all_to_all(collected[0], 'kv', split_axis=1, concat_axis=0, tiled=True)  29.5 us
    reshape x2, local copies, waits for them, and re-layouts, restack(): return jnp.transpose(ordered, (1, 0, 2, 3)).reshape(-1, columns)  19.7 us
    dot_general x8, matrix products, prefix_step(): jnp.einsum('gnqst,sgdt->gnqd', weights, value_part, preferred_element_typ...  18.6 us
  transfers between devices with their start and end apart: 6, of which 4 were waited for; matrix products, arithmetic and copies ran while one was open for 19% of the time, Pallas kernels for 0%

profile of v1, /device:TPU:1, one launch (start us, length us, event | category | flops | bytes accessed | tf_op | source)
XLA Modules:
  0.0 828.9 jit_solution(13409117487098557881)
XLA Ops:
  16.2 8.6 %all-to-all-start.1 = ((bf16[2,32,1,80,128]{4,3,0,2,1:T(8,128)(2,1)}), bf16[2,32,1,80,128]{4,3,0,2,1:T(8,128)(2,1)S(1)}, u32[]{:S(2)}, u32[]{:S(2)}) async-start(bf16[2,32,1,80,128]{4,3,0,2,1:T(8,128)(2,1)} %fusion.67), calls=%async_computation.1 | async-start | bytes 2621440 | tf_op jit(solution)/shard_map/all_to_all | solution.py:172
  32.4 40.8 %all-gather.9.cloned.1.call-done = bf16[16,20,3840]{2,1,0:T(8,128)(2,1)} async-done(((bf16[1,20,3840]{2,1,0:T(8,128)(2,1)}), bf16[16,20,3840]{2,1,0:T(8,128)(2,1)}) %all-gather.9.cloned.1.call-update) | async-done | bytes 2457616 | tf_op jit(solution)/shard_map/all_gather | solution.py:112
  73.2 6.5 all_to_all.27
  79.7 4.1 copy.47
  83.8 4.4 all-to-all-start
  89.8 4.4 copy.46
  101.0 29.5 %all-to-all-done = bf16[320,8,480]{2,0,1:T(8,128)(2,1)} async-done(((bf16[320,8,480]{2,0,1:T(8,128)(2,1)}), bf16[320,8,480]{2,0,1:T(8,128)(2,1)}, u32[]{:S(2)}, u32[]{:S(2)}) %all-to-all-start) | async-done | bytes 2457632 | tf_op jit(solution)/shard_map/all_to_all | solution.py:116
  130.5 3.2 copy.48
  136.5 5.5 reshape.470
  142.0 4.2 fusion.54
  151.0 63.4 %while.16 = (s32[]{:T(128)}, f32[1,4,512]{2,1,0:T(4,128)S(1)}, f32[1,4,512]{2,1,0:T(4,128)S(1)}, f32[1,4,512,80]{2,3,1,0:T(8,128)}, pred[8,4]{1,0:T(8,128)(4,1)S...) while((s32[]{:T(128)}, f32[1,4,512]{2,1,0:T(4,128)S(1)}, ...), condition=%wide.region_14.15_spmd.clone.clone, body=%wide.region_11.14_spmd.clone.clone.sunk | while | flops 351253504 | bytes 20843776 | solution.py:204
  218.7 16.5 %all_to_all.31 = bf16[320,8,1728]{2,1,0:T(8,128)(2,1)} reshape(bf16[16,20,13824]{2,1,0:T(8,128)(2,1)} %all-gather.11.cloned.1.call-done) | data formatting | bytes 17694720 | tf_op jit(solution)/shard_map/all_to_all | solution.py:117
  235.2 9.0 %copy.54 = bf16[320,8,1728]{2,0,1:T(8,128)(2,1)} copy(bf16[320,8,1728]{2,1,0:T(8,128)(2,1)} %all_to_all.31) | data formatting | bytes 17694720 | tf_op jit(solution)/shard_map/all_to_all | solution.py:117
  244.3 207.0 %all_to_all.37 = bf16[320,8,1728]{2,0,1:T(8,128)(2,1)} all-to-all(bf16[320,8,1728]{2,0,1:T(8,128)(2,1)} %copy.54), channel_id=1, replica_groups=mesh['blk'=16,'kv'=8] {'kv'}, dimensions={1} | all-to-all | bytes 17694720 | tf_op jit(solution)/shard_map/all_to_all | solution.py:117
  451.3 12.3 %copy.55 = bf16[320,8,1728]{2,1,0:T(8,128)(2,1)} copy(bf16[320,8,1728]{2,0,1:T(8,128)(2,1)} %all_to_all.37) | data formatting | bytes 17694720 | tf_op jit(solution)/shard_map/all_to_all | solution.py:117
  463.6 10.4 %copy.56 = bf16[16,8,20,1728]{3,2,1,0:T(8,128)(2,1)} copy(bf16[16,8,20,1728]{3,1,2,0:T(8,128)(2,1)} %bitcast.200) | data formatting | bytes 17694720 | tf_op jit(solution)/shard_map/transpose | solution.py:86
  474.0 14.2 %reshape.479 = bf16[2560,1728]{1,0:T(8,128)(2,1)} reshape(bf16[16,8,20,1728]{3,2,1,0:T(8,128)(2,1)} %copy.56) | data formatting | bytes 17694720 | tf_op jit(solution)/shard_map/reshape | solution.py:86
  488.2 233.7 %all-gather.7.cloned.1.call-done = bf16[4096,2560]{1,0:T(8,128)(2,1)} async-done(((bf16[512,2560]{1,0:T(8,128)(2,1)}), bf16[4096,2560]{1,0:T(8,128)(2,1)}) %all-gather.7.cloned.1.call-update) | async-done | bytes 20971536 | tf_op jit(solution)/shard_map/all_gather | solution.py:213
  721.9 13.1 %reduce_sum.101 = bf16[512,2560]{1,0:T(8,128)(2,1)} reduce(bf16[8,512,2560]{2,1,0:T(8,128)(2,1)} %bitcast.201, bf16[]{:T(256)} %constant.118.clone.1), dimensions={0}, to_apply=%region_15.16 | reduce | flops 9175040 | bytes 23592962 | tf_op jit(solution)/shard_map/reduce_sum | solution.py:213
  735.0 4.4 copy.53
  739.4 3.7 fusion.44
  743.2 9.2 %fusion.56 = f32[512,1728]{0,1:T(8,128)S(1)} fusion(bf16[2560,1728]{1,0:T(8,128)(2,1)} %reshape.479, bf16[512,2560]{0,1:T(8,128)(2,1)S(1)} %get-tuple-element.174, f32[2560]{0:T(1024)S(1)} %copy-done.7, f32[512]{0:T(512)S(1)} %add_rsqrt_fusion), kind=kOutput, calls=%fused_computation.67 | convolution fusion | flops 4535091200 | bytes 15020032 | tf_op jit(solution)/shard_map/dot_general | solution.py:218
  752.4 4.4 convolution_convert_fusion
  756.9 63.4 %reduce-scatter.2.cloned.1.call-done = bf16[512,320]{0,1:T(8,128)(2,1)} async-done(((bf16[512,2560]{0,1:T(8,128)(2,1)}), bf16[512,320]{0,1:T(8,128)(2,1)}) %reduce-scatter.2.cloned.1.call-update) | async-done | bytes 327696 | tf_op jit(solution)/shard_map/reduce_scatter | solution.py:222
  (218 shorter events, 101.5 us)
Async XLA Ops:
  6.5 209.0 %copy-start = (bf16[320,2560]{1,0:T(8,128)(2,1)S(1)}, bf16[320,2560]{1,0:T(8,128)(2,1)}, u32[]{:S(2)}) copy-start(bf16[320,2560]{1,0:T(8,128)(2,1)} %param.24) | copy-start | bytes 4915204
  6.5 66.6 %all-gather.9.cloned.1.call-start = ((), (), s32[]{:S(2)}) async-start(), calls=%async_computation.6 | async-start | bytes 3133440 | tf_op jit(solution)/shard_map/all_gather | solution.py:112
  16.2 16.1 %copy-start.5 = (s32[128]{0:T(128)S(1)}, s32[128]{0:T(128)}, u32[]{:S(2)}) copy-start(s32[128]{0:T(128)} %param.27) | copy-start | bytes 1540
  16.2 67.6 %all-to-all-start.1 = ((bf16[2,32,1,80,128]{4,3,0,2,1:T(8,128)(2,1)}), bf16[2,32,1,80,128]{4,3,0,2,1:T(8,128)(2,1)S(1)}, u32[]{:S(2)}, u32[]{:S(2)}) async-start(bf16[2,32,1,80,128]{4,3,0,2,1:T(8,128)(2,1)} %fusion.67), calls=%async_computation.1 | async-start | bytes 2621440 | tf_op jit(solution)/shard_map/all_to_all | solution.py:172
  24.8 194.0 %all-gather.11.cloned.1.call-start = ((), (), s32[]{:S(2)}) async-start(), calls=%async_computation.7 | async-start | bytes 11280384 | tf_op jit(solution)/shard_map/all_gather | solution.py:113
  79.7 8.9 %copy-start.8 = (s32[16]{0:T(128)S(1)}, s32[16]{0:T(128)}, u32[]{:S(2)}) copy-start(s32[16]{0:T(128)} %param.28) | copy-start | bytes 196
  79.7 9.4 %copy-start.9 = (s32[16]{0:T(128)S(1)}, s32[16]{0:T(128)}, u32[]{:S(2)}) copy-start(s32[16]{0:T(128)} %param.29) | copy-start | bytes 196
  83.8 46.7 %all-to-all-start = ((bf16[320,8,480]{2,0,1:T(8,128)(2,1)}), bf16[320,8,480]{2,0,1:T(8,128)(2,1)}, u32[]{:S(2)}, u32[]{:S(2)}) async-start(bf16[320,8,480]{2,0,1:T(8,128)(2,1)} %copy.47), calls=%async_computation | async-start | bytes 5242880 | tf_op jit(solution)/shard_map/all_to_all | solution.py:116
  88.2 633.7 %all-gather.7.cloned.1.call-start = ((), (), s32[]{:S(2)}) async-start(), calls=%async_computation.5 | async-start | bytes 23592960 | tf_op jit(solution)/shard_map/all_gather | solution.py:213
  136.5 5.5 copy-start.6
  153.2 3.0 copy-start.3
  161.1 3.0 copy-start.3
  169.0 3.0 copy-start.3
  176.8 3.0 copy-start.3
  184.7 3.0 copy-start.3
  192.5 3.0 copy-start.3
  200.4 3.0 copy-start.3
  208.2 3.0 copy-start.3
  218.7 601.6 %reduce-scatter.2.cloned.1.call-start = ((), (), s32[]{:S(2)}) async-start(), calls=%async_computation.4 | async-start | bytes 2949120 | tf_op jit(solution)/shard_map/reduce_scatter | solution.py:222
  739.4 3.8 copy-start.7
  739.4 13.0 %slice-start = ((s8[4423680]{0:T(1024)(128)(4,1)}), s8[4194304]{0:T(1024)(128)(4,1)S(1)}, s32[]{:S(2)}) async-start(s8[4423680]{0:T(1024)(128)(4,1)} %bitcast.213), calls=%async_computation.8 | async-start | bytes 8388608
  743.1 9.2 %copy-start.2 = (bf16[512,2560]{0,1:T(8,128)(2,1)}, bf16[512,2560]{0,1:T(8,128)(2,1)S(1)}, u32[]{:S(2)}) copy-start(bf16[512,2560]{0,1:T(8,128)(2,1)S(1)} %get-tuple-element.174) | copy-start | bytes 7864324
  743.1 9.2 %slice-start.1 = ((s8[4423680]{0:T(1024)(128)(4,1)}), s8[229376]{0:T(1024)(128)(4,1)S(1)}, s32[]{:S(2)}) async-start(s8[4423680]{0:T(1024)(128)(4,1)} %bitcast.213), calls=%async_computation.9 | async-start | bytes 458752
  752.4 69.8 %copy-start.1 = (bf16[320,2560]{1,0:T(8,128)(2,1)S(1)}, bf16[320,2560]{1,0:T(8,128)(2,1)}, u32[]{:S(2)}) copy-start(bf16[320,2560]{1,0:T(8,128)(2,1)} %param.24) | copy-start | bytes 4915204
  (8 other events, 6.8 us)
Sparse Core Ops, SparseCore 0:
  10.9 62.2 all-gather.8
  75.6 91.7 all-gather.10
  218.8 503.0 all-gather.6
  757.0 63.2 reduce-scatter.1
